TPU v7x, 32 devices: a whole 2x2x4 slice. The times are simulated.
32 devices in a mesh: fish: 2 (over y), img: 16 (over z, x, core).
Axes of the slice: x: 2, y: 2, z: 4, core: 2. Of those that a mesh axis runs over, the one named last changes fastest.
Arguments:
- img_feat: bfloat16 [64, 16384], P(None, ('fish', 'img')), parts along dimension 1, may hold values from -80 to 80
- mdl_feat: bfloat16 [64, 2048], P(None, ('fish', 'img')), parts along dimension 1, may hold values from -80 to 80
- img_mass: float32 [16384], P(('fish', 'img')), parts along dimension 0, may hold values from 0.5 to 2
- mdl_mass: float32 [2048], P('fish'), parts along dimension 0, may hold values from 0.5 to 2
Outputs:
- grad_img: float32 [64, 16384], P(None, ('fish', 'img')), parts along dimension 1
- grad_mdl: float32 [64, 2048], P(None, ('fish', 'img')), parts along dimension 1
There are 2 independent parts, one for each index of `fish`. A program takes and returns all parts, laid end to end along the dimension named above; each array names one. Nothing has to cross between parts.
All inputs are finite; a program needn't handle non-finite values.
Results may differ from a plain program's by a relative error of at most 0.005.
Values may be sent and summed in bfloat16 or wider, within the bound.
No kernel may reach another device: no remote copies, remote signals or barrier semaphores. Data moves between devices by JAX's collectives and lax.ppermute only.
A program may use at most 64 MiB of HBM per device.

v0:
```python
import jax
import jax.numpy as jnp
from jax import lax
from jax.sharding import PartitionSpec as P

FEAT = 64
ITERS = 4
inv_temp = 20.0


def normalize(features):
    wide = features.astype(jnp.float32)
    guarded = jnp.mean(wide * wide, axis=0, keepdims=True) + 1e-06
    return (wide * lax.rsqrt(guarded)).astype(jnp.bfloat16)


def kernel_tile(imaged_unit, model_slice, factor):
    scores = lax.dot_general(
        imaged_unit, model_slice, (((0,), (0,)), ((), ())), preferred_element_type=jnp.float32
    )
    return jnp.exp(scores * factor).astype(jnp.bfloat16)


def shards(img_feat, mdl_feat, img_mass, mdl_mass):
    factor = inv_temp / FEAT
    imaged_unit = normalize(img_feat)
    model_unit = lax.all_gather(normalize(mdl_feat), "img", axis=1, tiled=True)
    total_model = model_unit.shape[1]
    share = mdl_feat.shape[1]
    local_rows = img_feat.shape[1]
    offset = lax.axis_index("img") * share
    kernel = kernel_tile(imaged_unit, model_unit, factor)
    col_scale = jnp.ones((total_model,), jnp.float32)
    col_low = col_scale.astype(jnp.bfloat16)
    row_scale = jnp.ones((local_rows,), jnp.float32)
    for iteration in range(ITERS):
        row_scale = img_mass / jnp.dot(kernel, col_low, preferred_element_type=jnp.float32)
        partial_cols = jnp.dot(
            row_scale.astype(jnp.bfloat16), kernel, preferred_element_type=jnp.float32
        )
        col_scale = mdl_mass / lax.psum(partial_cols, "img")
        col_low = col_scale.astype(jnp.bfloat16)
    weighted = (model_unit.astype(jnp.float32) * col_scale[None, :]).astype(jnp.bfloat16)
    grad_img = -(
        lax.dot_general(
            weighted, kernel, (((1,), (1,)), ((), ())), preferred_element_type=jnp.float32
        )
        * row_scale[None, :]
    )
    row_feat = (imaged_unit.astype(jnp.float32) * row_scale[None, :]).astype(jnp.bfloat16)
    summed = lax.psum_scatter(
        lax.dot_general(
            kernel, row_feat, (((0,), (1,)), ((), ())), preferred_element_type=jnp.float32
        ),
        "img",
        scatter_dimension=0,
        tiled=True,
    )
    own_scale = lax.dynamic_slice_in_dim(col_scale, offset, share, 0)
    grad_mdl = -(summed * own_scale[:, None]).T
    return (grad_img, grad_mdl)


def solution(mesh):
    placed = (P(None, ("fish", "img")), P(None, ("fish", "img")), P(("fish", "img")), P("fish"))
    return jax.shard_map(
        shards,
        mesh=mesh,
        in_specs=placed,
        out_specs=(P(None, ("fish", "img")), P(None, ("fish", "img"))),
        check_vma=False,
    )
```

profile of v0, /device:TPU:0, one launch (start us, length us, event | category | flops | bytes accessed | tf_op | source)
XLA Modules:
  0.0 188.4 jit_solution(11212692938415362139)
XLA Ops:
  7.2 0.0 reduce-scatter.2.cloned.1.call-start
  7.2 0.8 copy.7
  8.0 0.1 fusion.8
  8.1 0.1 fusion.9
  8.2 23.8 %all_gather.3 = bf16[64,1024]{0,1:T(8,128)(2,1)S(1)} all-gather(bf16[64,64]{0,1:T(8,128)(2,1)S(1)} %fusion.9), channel_id=1, replica_groups=mesh['fish'=2,'img'=16] {'img'}, dimensions={1}, use_global_device_ids=true | all-gather | bytes 139264 | tf_op jit(solution)/shard_map/all_gather | solution.py:27
  32.0 0.9 fusion.2
  32.9 0.0 copy-start.2
  32.9 1.3 exponential_convert_fusion
  34.2 0.0 copy-start.1
  34.2 0.4 fusion.10
  34.6 0.0 copy-done.2
  34.7 0.2 fusion.14
  34.9 29.8 %psum.28 = f32[1024]{0:T(1024)S(1)} all-reduce(f32[1024]{0:T(1024)S(1)} %bitcast.28), channel_id=1, replica_groups=mesh['fish'=2,'img'=16] {'img'}, use_global_device_ids=true, to_apply=%region_2.0 | all-reduce | flops 1024 | bytes 8192 | tf_op jit(solution)/shard_map/psum | solution.py:41
  64.7 0.0 copy-done.1
  64.7 0.4 fusion.15
  65.1 0.3 fusion.16
  65.4 29.5 %psum.29 = f32[1024]{0:T(1024)S(1)} all-reduce(f32[1024]{0:T(1024)S(1)} %bitcast.29), channel_id=1, replica_groups=mesh['fish'=2,'img'=16] {'img'}, use_global_device_ids=true, to_apply=%region_3.0 | all-reduce | flops 1024 | bytes 8192 | tf_op jit(solution)/shard_map/psum | solution.py:41
  94.9 0.4 fusion.17
  95.3 0.0 copy-start
  95.3 0.2 fusion.18
  95.5 29.5 %psum.30 = f32[1024]{0:T(1024)S(1)} all-reduce(f32[1024]{0:T(1024)S(1)} %bitcast.30), channel_id=1, replica_groups=mesh['fish'=2,'img'=16] {'img'}, use_global_device_ids=true, to_apply=%region_4.0 | all-reduce | flops 1024 | bytes 8192 | tf_op jit(solution)/shard_map/psum | solution.py:41
  125.0 0.4 fusion.19
  125.4 0.0 copy-done
  125.4 1.3 fusion.4
  126.7 0.0 reduce-scatter.2.cloned.1.call-update
  126.7 0.2 fusion.20
  127.0 29.5 %psum.31 = f32[1024]{0:T(1024)S(1)} all-reduce(f32[1024]{0:T(1024)S(1)} %bitcast.31), channel_id=1, replica_groups=mesh['fish'=2,'img'=16] {'img'}, use_global_device_ids=true, to_apply=%region_5.0 | all-reduce | flops 1024 | bytes 8192 | tf_op jit(solution)/shard_map/psum | solution.py:41
  156.5 0.1 dynamic_slice.3
  156.6 1.3 fusion
  157.9 22.0 %reduce-scatter.2.cloned.1.call-done = f32[64,64]{1,0:T(8,128)} async-done(((f32[1024,64]{1,0:T(8,128)}), f32[64,64]{1,0:T(8,128)}) %reduce-scatter.2.cloned.1.call-update) | async-done | bytes 16400 | tf_op jit(solution)/shard_map/reduce_scatter | solution.py:51
  180.0 0.8 negate_bitcast_fusion
  180.8 0.7 copy.8
  (17 shorter events, 0.1 us)
Async XLA Ops:
  7.2 172.8 %reduce-scatter.2.cloned.1.call-start = ((), (), s32[]{:S(2)}) async-start(), calls=%async_computation.1 | async-start | bytes 557056 | tf_op jit(solution)/shard_map/reduce_scatter | solution.py:51
  32.9 1.7 copy-start.2
  34.2 30.5 %copy-start.1 = (f32[1024]{0:T(1024)S(1)}, f32[1024]{0:T(1024)}, u32[]{:S(2)}) copy-start(f32[1024]{0:T(1024)} %param.7) | copy-start | bytes 12292
  95.3 30.1 %copy-start = (bf16[64,512]{1,0:T(8,128)(2,1)S(1)}, bf16[64,512]{1,0:T(8,128)(2,1)}, u32[]{:S(2)}) copy-start(bf16[64,512]{1,0:T(8,128)(2,1)} %param.4) | copy-start | bytes 196612
Sparse Core Ops, SparseCore 0:
  126.9 53.0 reduce-scatter.1
where the time goes:
time: 189 us; the launch traced here: 188 us
  blocking collectives  142 us (75%)
  waiting for transfers between devices  22.1 us (12%)
  between operations  14.1 us (7%)
  matrix products  6.44 us (3%)
  other arithmetic  1.98 us (1%)
    psum x4, blocking collectives, shards(): col_scale = mdl_mass / lax.psum(partial_cols, 'img')  118 us
    all_gather x1, blocking collectives, shards(): model_unit = lax.all_gather(normalize(mdl_feat), 'img', axis=1, tiled=True)  23.8 us
    reduce_scatter x1, waiting for transfers between devices, shards(): lax.psum_scatter(lax.dot_general(kernel, row_feat, (((0,), (1,)), ((), ()...  22 us
  transfers between devices with their start and end apart: 1, of which 1 were waited for; matrix products, arithmetic and copies ran while one was open for 1% of the time, Pallas kernels for 0%

commit v1 on v0

--- a/solution.py
+++ b/solution.py
@@ -38,7 +38,11 @@
         partial_cols = jnp.dot(
             row_scale.astype(jnp.bfloat16), kernel, preferred_element_type=jnp.float32
         )
-        col_scale = mdl_mass / lax.psum(partial_cols, "img")
+
+        def _meet_forms(base_x):
+            return jax.lax.all_gather(base_x, axis_name="img").sum(axis=0)
+
+        col_scale = mdl_mass / _meet_forms(partial_cols)
         col_low = col_scale.astype(jnp.bfloat16)
     weighted = (model_unit.astype(jnp.float32) * col_scale[None, :]).astype(jnp.bfloat16)
     grad_img = -(

time: 189 us -> 155 us (0.82)
  blocking collectives: 142 us -> 96.8 us
  waiting for transfers between devices: 22.1 us -> 33.7 us
    psum x4 -> x0, blocking collectives: 118 us -> none  [shards(): col_scale = mdl_mass / lax.psum(partial_cols, 'img')]
    all_gather x0 -> x4, blocking collectives: none -> 73 us  [_meet_forms(): return jax.lax.all_gather(base_x, axis_name='img').sum(axis=0)]
    reduce_scatter x1, waiting for transfers between devices: 22 us -> 33.7 us  [shards(): lax.psum_scatter(lax.dot_general(kernel, row_feat, (((0,), (1,)), ((), ()...]
where the time goes in v1:
time: 155 us
  blocking collectives  96.8 us (62%)
  waiting for transfers between devices  33.7 us (22%)
  between operations  14.2 us (9%)
  matrix products  6.42 us (4%)
  other arithmetic  2.03 us (1%)
  local copies, waits for them, and re-layouts  1.72 us (1%)
    all_gather x4, blocking collectives, _meet_forms(): return jax.lax.all_gather(base_x, axis_name='img').sum(axis=0)  73 us
    reduce_scatter x1, waiting for transfers between devices, shards(): lax.psum_scatter(lax.dot_general(kernel, row_feat, (((0,), (1,)), ((), ()...  33.7 us
    all_gather x1, blocking collectives, shards(): model_unit = lax.all_gather(normalize(mdl_feat), 'img', axis=1, tiled=True)  23.8 us
  transfers between devices with their start and end apart: 1, of which 1 were waited for; matrix products, arithmetic and copies ran while one was open for 1% of the time, Pallas kernels for 0%

profile of v1, /device:TPU:0, one launch (start us, length us, event | category | flops | bytes accessed | tf_op | source)
XLA Modules:
  0.0 154.9 jit_solution(436602811876738528)
XLA Ops:
  7.2 0.0 reduce-scatter.2.cloned.1.call-start
  7.2 0.8 copy.9
  8.0 0.1 fusion.8
  8.1 0.1 fusion.9
  8.2 23.8 %all_gather.27 = bf16[64,1024]{0,1:T(8,128)(2,1)S(1)} all-gather(bf16[64,64]{0,1:T(8,128)(2,1)S(1)} %fusion.9), channel_id=1, replica_groups=mesh['fish'=2,'img'=16] {'img'}, dimensions={1}, use_global_device_ids=true | all-gather | bytes 139264 | tf_op jit(solution)/shard_map/all_gather | solution.py:27
  32.0 0.9 fusion.2
  32.9 0.0 copy-start.2
  32.9 1.3 exponential_convert_fusion
  34.2 0.0 copy-start.1
  34.2 0.4 fusion.10
  34.6 0.0 copy-done.2
  34.7 0.2 fusion.14
  34.9 17.6 %all-gather = f32[16384]{0:T(1024)S(1)} all-gather(f32[1024]{0:T(1024)S(1)} %bitcast.29), channel_id=2, replica_groups=mesh['fish'=2,'img'=16] {'img'}, dimensions={0}, use_global_device_ids=true | all-gather | bytes 69632 | tf_op jit(solution)/shard_map/all_gather | solution.py:43
  52.5 0.0 copy-done.1
  52.6 0.4 fusion.15
  53.0 0.3 fusion.16
  53.2 18.9 %all-gather.1 = f32[16384]{0:T(1024)S(1)} all-gather(f32[1024]{0:T(1024)S(1)} %bitcast.30), channel_id=3, replica_groups=mesh['fish'=2,'img'=16] {'img'}, dimensions={0}, use_global_device_ids=true | all-gather | bytes 69632 | tf_op jit(solution)/shard_map/all_gather | solution.py:43
  72.2 0.4 fusion.17
  72.6 0.0 copy-start
  72.6 0.2 fusion.18
  72.9 17.6 %all-gather.2 = f32[16384]{0:T(1024)S(1)} all-gather(f32[1024]{0:T(1024)S(1)} %bitcast.31), channel_id=4, replica_groups=mesh['fish'=2,'img'=16] {'img'}, dimensions={0}, use_global_device_ids=true | all-gather | bytes 69632 | tf_op jit(solution)/shard_map/all_gather | solution.py:43
  90.6 0.4 fusion.19
  90.9 0.0 copy-done
  91.0 1.3 fusion.4
  92.2 0.0 reduce-scatter.2.cloned.1.call-update
  92.3 0.2 fusion.20
  92.5 18.9 %all-gather.3 = f32[16384]{0:T(1024)S(1)} all-gather(f32[1024]{0:T(1024)S(1)} %bitcast.28), channel_id=5, replica_groups=mesh['fish'=2,'img'=16] {'img'}, dimensions={0}, use_global_device_ids=true | all-gather | bytes 69632 | tf_op jit(solution)/shard_map/all_gather | solution.py:43
  111.5 0.1 dynamic_slice.3
  111.6 1.3 fusion
  112.9 33.7 %reduce-scatter.2.cloned.1.call-done = f32[64,64]{1,0:T(8,128)} async-done(((f32[1024,64]{1,0:T(8,128)}), f32[64,64]{1,0:T(8,128)}) %reduce-scatter.2.cloned.1.call-update) | async-done | bytes 16400 | tf_op jit(solution)/shard_map/reduce_scatter | solution.py:55
  146.6 0.8 negate_bitcast_fusion
  147.4 0.7 copy.10
  (25 shorter events, 0.3 us)
Async XLA Ops:
  7.2 139.4 %reduce-scatter.2.cloned.1.call-start = ((), (), s32[]{:S(2)}) async-start(), calls=%async_computation.1 | async-start | bytes 557056 | tf_op jit(solution)/shard_map/reduce_scatter | solution.py:55
  32.9 1.7 %copy-start.2 = (f32[512]{0:T(512)S(1)}, f32[512]{0:T(512)}, u32[]{:S(2)}) copy-start(f32[512]{0:T(512)} %param.6) | copy-start | bytes 6148
  34.2 18.3 %copy-start.1 = (f32[1024]{0:T(1024)S(1)}, f32[1024]{0:T(1024)}, u32[]{:S(2)}) copy-start(f32[1024]{0:T(1024)} %param.7) | copy-start | bytes 12292
  72.6 18.3 %copy-start = (bf16[64,512]{1,0:T(8,128)(2,1)S(1)}, bf16[64,512]{1,0:T(8,128)(2,1)}, u32[]{:S(2)}) copy-start(bf16[64,512]{1,0:T(8,128)(2,1)} %param.4) | copy-start | bytes 196612
Sparse Core Ops, SparseCore 0:
  92.4 54.1 reduce-scatter.1
